TPU v7x, 512 devices: a whole 4x4x16 slice. The times are simulated.
512 devices in a mesh: dp: 64 (over y_lo, z, core), blk: 8 (over y_hi, x).
Axes of the slice: x: 4, y: 4 (y_hi: 2, y_lo: 2; y = y_hi * 2 + y_lo), z: 16, core: 2. Of those that a mesh axis runs over, the one named last changes fastest.
Arguments:
- resid: bfloat16 [2048, 2048], P('dp'), may hold values from -40 to 40
- queries: bfloat16 [2048, 16, 128], P('dp', 'blk'), may hold values from -60 to 60
- new_kv: bfloat16 [2048, 2, 8, 128], P('dp', None, 'blk'), may hold values from -6 to 6
- prefix_pool: bfloat16 [2048, 128, 2, 8, 128], P('dp', None, None, 'blk'), may hold values from -6 to 6
- page_table: int32 [64, 32], P('dp'), may hold values from 0 to 31, each once within a row
- prompt_len: int32 [64], P('dp'), may hold values from 1 to 4096, 131072 in all
- tail_pool: bfloat16 [1024, 128, 2, 8, 128], P('dp', None, None, 'blk'), may hold values from -6 to 6
- tail_len: int32 [64, 16], P('dp'), may hold values from 1 to 128, 1024 in all within a row
- migration: int32 [1024], replicated, may hold values from 0 to 1023, each once
- out_w: bfloat16 [2048, 2048], P('blk'), may hold values from -0.125 to 0.125
- mlp_gain: bfloat16 [2048], replicated, may hold values from 0.099609375 to 1.8984375
- gate_w: bfloat16 [2048, 6144], P('blk', 'dp'), may hold values from -0.125 to 0.125
- up_w: bfloat16 [2048, 6144], P('blk', 'dp'), may hold values from -0.125 to 0.125
- down_w: bfloat16 [6144, 2048], P('dp', 'blk'), may hold values from -0.078125 to 0.078125
- final_gain: bfloat16 [2048], P('blk'), may hold values from 0.099609375 to 1.8984375
- score_w: bfloat16 [2048], P('blk'), may hold values from -0.125 to 0.125
Outputs:
- hidden_out: bfloat16 [2048, 2048], P('dp', 'blk')
- score: float32 [2048], P('dp')
Inputs may be any that keep to these rules, and one draw needn't show every extreme that they name: `page_table`: each row lists every page of the device's pool once. `migration`: names every continuation once.
All inputs are finite; a program needn't handle non-finite values. No bound on the sum of `prompt_len` on one device may be relied on, other than what follows from the above.
Results may differ from a plain program's by a relative error of at most 0.012.
Values may be sent and summed in bfloat16 or wider, within the bound.
A program may use at most 64 MiB of HBM per device.

v0:
```python
import math
import jax
import jax.numpy as jnp
from jax import lax
from jax.sharding import PartitionSpec as P

D = 2048
NEW = 2
NEG = -1e30
EPS = 1e-06


def attend_prompt(queries, pool, table, prompt_len, tails, tail_len, pairs):
    token_rows, heads, width = queries.shape
    groups = pairs.shape[2]
    repeat = heads // groups
    conts = tails.shape[0]
    fresh = token_rows // conts
    prefix = jnp.take(pool, table, axis=0).reshape(-1, 2, groups, width)
    span = prefix.shape[0]
    grouped = queries.reshape(conts, fresh, groups, repeat, width)
    recent = pairs.reshape(conts, fresh, 2, groups, width)
    factor = 1.0 / math.sqrt(width)
    pre_scores = (
        jnp.einsum("cngrd,pgd->gcnrp", grouped, prefix[:, 0], preferred_element_type=jnp.float32)
        * factor
    )
    tail_scores = (
        jnp.einsum("cngrd,ctgd->gcnrt", grouped, tails[:, :, 0], preferred_element_type=jnp.float32)
        * factor
    )
    new_scores = (
        jnp.einsum(
            "cngrd,cmgd->gcnrm", grouped, recent[:, :, 0], preferred_element_type=jnp.float32
        )
        * factor
    )
    pre_mask = (jnp.arange(span) < prompt_len)[None, None, None, None, :]
    tail_mask = (jnp.arange(tails.shape[1])[None, :] < tail_len[:, None])[None, :, None, None, :]
    new_mask = (jnp.arange(fresh)[None, :] <= jnp.arange(fresh)[:, None])[None, None, :, None, :]
    pre_scores = jnp.where(pre_mask, pre_scores, NEG)
    tail_scores = jnp.where(tail_mask, tail_scores, NEG)
    new_scores = jnp.where(new_mask, new_scores, NEG)
    highest = jnp.maximum(
        jnp.maximum(jnp.max(pre_scores, -1), jnp.max(tail_scores, -1)), jnp.max(new_scores, -1)
    )[..., None]
    pre_weights = jnp.where(pre_mask, jnp.exp(pre_scores - highest), 0.0)
    tail_weights = jnp.where(tail_mask, jnp.exp(tail_scores - highest), 0.0)
    new_weights = jnp.where(new_mask, jnp.exp(new_scores - highest), 0.0)
    total = jnp.sum(pre_weights, -1) + jnp.sum(tail_weights, -1) + jnp.sum(new_weights, -1)
    mixed = jnp.einsum(
        "gcnrp,pgd->cngrd",
        pre_weights.astype(jnp.bfloat16),
        prefix[:, 1],
        preferred_element_type=jnp.float32,
    )
    mixed = mixed + jnp.einsum(
        "gcnrt,ctgd->cngrd",
        tail_weights.astype(jnp.bfloat16),
        tails[:, :, 1],
        preferred_element_type=jnp.float32,
    )
    mixed = mixed + jnp.einsum(
        "gcnrm,cmgd->cngrd",
        new_weights.astype(jnp.bfloat16),
        recent[:, :, 1],
        preferred_element_type=jnp.float32,
    )
    mixed = mixed / jnp.transpose(total, (1, 2, 0, 3))[..., None]
    return mixed.reshape(token_rows, heads * width).astype(jnp.bfloat16)


def shards(
    resid,
    queries,
    new_kv,
    prefix_pool,
    page_table,
    prompt_len,
    tail_pool,
    tail_len,
    migration,
    out_w,
    mlp_gain,
    gate_w,
    up_w,
    down_w,
    final_gain,
    score_w,
):
    token_rows = resid.shape[0]
    attn = attend_prompt(
        queries, prefix_pool, page_table[0], prompt_len[0], tail_pool, tail_len[0], new_kv
    )
    partial_value = jnp.dot(attn, out_w, preferred_element_type=jnp.float32)
    mixed = lax.psum(partial_value.astype(jnp.bfloat16), "blk").astype(jnp.float32)
    middle = resid.astype(jnp.float32) + mixed
    normed = (
        middle
        * lax.rsqrt(jnp.mean(middle * middle, -1, keepdims=True) + EPS)
        * mlp_gain.astype(jnp.float32)
    ).astype(jnp.bfloat16)
    feat_width = gate_w.shape[0]
    units = gate_w.shape[1]
    block_index = lax.axis_index("blk")
    home_index = lax.axis_index("dp")
    feat_slice = lax.dynamic_slice_in_dim(normed, block_index * feat_width, feat_width, 1)
    middle_slice = lax.dynamic_slice_in_dim(middle, block_index * feat_width, feat_width, 1)
    piece = lax.all_gather(feat_slice, "dp", axis=0, tiled=True)
    partial_units = jnp.concatenate(
        [
            jnp.dot(piece, gate_w, preferred_element_type=jnp.float32),
            jnp.dot(piece, up_w, preferred_element_type=jnp.float32),
        ],
        axis=1,
    )
    summed = lax.psum(partial_units.astype(jnp.bfloat16), "blk").astype(jnp.float32)
    hidden = (jax.nn.silu(summed[:, :units]) * summed[:, units:]).astype(jnp.bfloat16)
    source = (migration[:, None] * NEW + jnp.arange(NEW, dtype=jnp.int32)[None, :]).reshape(-1)
    term = jnp.dot(jnp.take(hidden, source, axis=0), down_w, preferred_element_type=jnp.float32)
    local_rows = source - home_index * token_rows
    own_rows = (local_rows >= 0) & (local_rows < token_rows)
    carried = jnp.take(middle_slice, jnp.clip(local_rows, 0, token_rows - 1), axis=0)
    moved = lax.psum_scatter(
        term + jnp.where(own_rows[:, None], carried, 0.0), "dp", scatter_dimension=0, tiled=True
    )
    weighted = final_gain.astype(jnp.float32) * score_w.astype(jnp.float32)
    squares, terms = lax.psum((jnp.sum(moved * moved, -1), jnp.sum(moved * weighted, -1)), "blk")
    score = terms * lax.rsqrt(squares / D + EPS)
    return (moved.astype(jnp.bfloat16), score)


def solution(mesh):
    return jax.shard_map(
        shards,
        mesh=mesh,
        in_specs=(
            P("dp", None),
            P("dp", "blk", None),
            P("dp", None, "blk", None),
            P("dp", None, None, "blk", None),
            P("dp", None),
            P("dp"),
            P("dp", None, None, "blk", None),
            P("dp", None),
            P(),
            P("blk", None),
            P(),
            P("blk", "dp"),
            P("blk", "dp"),
            P("dp", "blk"),
            P("blk"),
            P("blk"),
        ),
        out_specs=(P("dp", "blk"), P("dp")),
        check_vma=False,
    )
```

profile of v0, /device:TPU:8, one launch (start us, length us, event | category | flops | bytes accessed | tf_op | source)
XLA Modules:
  0.0 631.7 jit_solution(11279439814743314583)
XLA Ops:
  7.2 0.8 fusion.25
  9.4 6.2 gather_fusion
  15.5 3.6 copy.69
  19.3 2.3 fusion.31
  22.7 2.0 broadcast_select_fusion
  24.7 1.3 copy-done.2
  27.9 1.6 fusion.11
  29.8 2.0 fusion.6
  31.9 0.9 convolution_convert_fusion.2
  32.9 0.8 dynamic-slice
  33.6 102.1 %all-reduce.4.cloned.1.call-done = bf16[32,2048]{1,0:T(8,128)(2,1)} async-done(((bf16[32,2048]{1,0:T(8,128)(2,1)}), bf16[32,2048]{1,0:T(8,128)(2,1)}) %all-reduce.4.cloned.1.call-update) | async-done | bytes 131088 | tf_op jit(solution)/shard_map/psum | solution.py:96
  135.7 1.1 convert_add_fusion
  138.4 119.5 %all-gather.2.cloned.1.call-done = bf16[2048,256]{1,0:T(8,128)(2,1)} async-done(((bf16[32,256]{1,0:T(8,128)(2,1)}), bf16[2048,256]{1,0:T(8,128)(2,1)}) %all-gather.2.cloned.1.call-update) | async-done | bytes 1048592 | tf_op jit(solution)/shard_map/all_gather | solution.py:109
  257.9 1.7 convolution_convert_fusion
  259.6 1.7 convolution_convert_fusion.1
  261.3 0.9 pad_maximum_fusion
  262.4 8.6 %gather_fusion.2 = f32[2048,256]{1,0:T(8,128)} fusion(f32[32,256]{1,0:T(8,128)S(1)} %get-tuple-element.7, s32[2048]{0:T(1024)S(1)} %broadcast_clamp_fusion), kind=kCustom, calls=%fused_computation.2 | custom fusion | bytes 4202496 | tf_op jit(solution)/shard_map/jit(_take)/gather | solution.py:123
  270.9 89.1 %all-reduce.6.cloned.1.call-done = bf16[2048,192]{0,1:T(8,128)(2,1)} async-done(((bf16[2048,192]{0,1:T(8,128)(2,1)}), bf16[2048,192]{0,1:T(8,128)(2,1)}) %all-reduce.6.cloned.1.call-update) | async-done | bytes 786448 | tf_op jit(solution)/shard_map/psum | solution.py:117
  360.0 1.3 convert_element_type.59
  361.9 6.2 gather_fusion.1
  368.1 4.9 convolution_add_fusion
  373.6 226.0 %reduce-scatter.2.cloned.1.call-done = f32[32,256]{1,0:T(8,128)} async-done(((f32[2048,256]{1,0:T(8,128)}), f32[32,256]{1,0:T(8,128)}) %reduce-scatter.2.cloned.1.call-update) | async-done | bytes 32784 | tf_op jit(solution)/shard_map/reduce_scatter | solution.py:124
  599.6 1.5 multiply_reduce_fusion.1
  601.1 23.5 %all-reduce = (f32[32]{0:T(128)S(1)}, f32[32]{0:T(128)S(1)}) all-reduce(f32[32]{0:T(128)S(1)} %get-tuple-element.3, f32[32]{0:T(128)S(1)} %get-tuple-element.2), channel_id=1, replica_groups=mesh['dp'=64,'blk'=8] {'blk'}, use_global_device_ids=true, to_apply=%region_11.12 | all-reduce | flops 64 | bytes 512 | tf_op jit(solution)/shard_map/psum | solution.py:128
  (74 shorter events, 7.5 us)
Async XLA Ops:
  7.2 2.2 copy-start
  7.2 128.6 %all-reduce.4.cloned.1.call-start = ((), (), s32[]{:S(2)}) async-start(), calls=%async_computation.1 | async-start | bytes 262144 | tf_op jit(solution)/shard_map/psum | solution.py:96
  15.5 3.7 copy-start.11
  15.5 3.7 copy-start.1
  19.3 2.3 copy-start.14
  19.3 2.9 copy-start.9
  24.7 1.4 copy-start.2
  26.6 1.0 copy-start.4
  27.9 3.9 copy-start.3
  29.8 105.9 %copy-start.5 = (bf16[32,2048]{1,0:T(8,128)(2,1)S(1)}, bf16[32,2048]{1,0:T(8,128)(2,1)}, u32[]{:S(2)}) copy-start(bf16[32,2048]{1,0:T(8,128)(2,1)} %param.16) | copy-start | bytes 393220
  29.8 107.7 %copy-start.10 = (s32[1024]{0:T(1024)S(1)}, s32[1024]{0:T(1024)}, u32[]{:S(2)}) copy-start(s32[1024]{0:T(1024)} %param.24) | copy-start | bytes 12292
  31.8 226.1 %copy-start.7 = (bf16[256,96]{0,1:T(8,128)(2,1)S(1)}, bf16[256,96]{0,1:T(8,128)(2,1)}, u32[]{:S(2)}) copy-start(bf16[256,96]{0,1:T(8,128)(2,1)} %param.28) | copy-start | bytes 147460
  32.8 226.8 %copy-start.8 = (bf16[256,96]{0,1:T(8,128)(2,1)S(1)}, bf16[256,96]{0,1:T(8,128)(2,1)}, u32[]{:S(2)}) copy-start(bf16[256,96]{0,1:T(8,128)(2,1)} %param.27) | copy-start | bytes 147460
  32.8 225.1 %all-gather.2.cloned.1.call-start = ((), (), s32[]{:S(2)}) async-start(), calls=%async_computation.2 | async-start | bytes 1064960 | tf_op jit(solution)/shard_map/all_gather | solution.py:109
  137.5 222.5 %all-reduce.6.cloned.1.call-start = ((), (), s32[]{:S(2)}) async-start(), calls=%async_computation.3 | async-start | bytes 1572864 | tf_op jit(solution)/shard_map/psum | solution.py:117
  262.2 337.3 %reduce-scatter.2.cloned.1.call-start = ((), (), s32[]{:S(2)}) async-start(), calls=%async_computation.4 | async-start | bytes 2129920 | tf_op jit(solution)/shard_map/reduce_scatter | solution.py:124
  361.8 6.2 copy-start.6
  372.9 0.7 copy-start.12
  372.9 0.7 copy-start.13
Sparse Core Ops, SparseCore 0:
  32.9 102.7 all-reduce.3
  138.7 119.1 all-gather.1
  262.4 97.6 all-reduce.5
  373.1 226.4 reduce-scatter.1
where the time goes:
time: 632 us
  waiting for transfers between devices  537 us (85%)
  local copies, waits for them, and re-layouts  31.4 us (5%)
  blocking collectives  23.5 us (4%)
  between operations  14.7 us (2%)
  matrix products  14.3 us (2%)
  other arithmetic  10.8 us (2%)
    reduce_scatter x1, waiting for transfers between devices, shards(): lax.psum_scatter(term + jnp.where(own_rows[:, None], carried, 0.0), 'dp',...  226 us
    all_gather x1, waiting for transfers between devices, shards(): piece = lax.all_gather(feat_slice, 'dp', axis=0, tiled=True)  120 us
    psum x1, waiting for transfers between devices, shards(): lax.psum(partial_value.astype(jnp.bfloat16), 'blk').astype(jnp.float32)  102 us
    psum x1, waiting for transfers between devices, shards(): lax.psum(partial_units.astype(jnp.bfloat16), 'blk').astype(jnp.float32)  89.1 us
    psum x1, blocking collectives, shards(): lax.psum((jnp.sum(moved * moved, -1), jnp.sum(moved * weighted, -1)), 'blk')  23.5 us
  transfers between devices with their start and end apart: 4, of which 4 were waited for; matrix products, arithmetic and copies ran while one was open for 2% of the time, Pallas kernels for 0%

commit v1 on v0

--- a/solution.py
+++ b/solution.py
@@ -8,6 +8,9 @@
 NEW = 2
 NEG = -1e30
 EPS = 1e-06
+part_threads = lambda payload: jnp.concatenate(
+    jax.lax.all_to_all(jnp.stack(jax.lax.axis_size("dp") * [payload]), "dp", 0, 0), axis=0
+)
 
 
 def attend_prompt(queries, pool, table, prompt_len, tails, tail_len, pairs):
@@ -106,7 +109,7 @@
     home_index = lax.axis_index("dp")
     feat_slice = lax.dynamic_slice_in_dim(normed, block_index * feat_width, feat_width, 1)
     middle_slice = lax.dynamic_slice_in_dim(middle, block_index * feat_width, feat_width, 1)
-    piece = lax.all_gather(feat_slice, "dp", axis=0, tiled=True)
+    piece = part_threads(feat_slice)
     partial_units = jnp.concatenate(
         [
             jnp.dot(piece, gate_w, preferred_element_type=jnp.float32),

time: 632 us -> 573 us (0.907)
  waiting for transfers between devices: 537 us -> 462 us
  starting transfers between devices: 0.16 us -> 14.6 us
    all_gather x1 -> x0, waiting for transfers between devices: 120 us -> none  [shards(): piece = lax.all_gather(feat_slice, 'dp', axis=0, tiled=True)]
    all_to_all x0 -> x1, waiting for transfers between devices: none -> 48.3 us  [jax.lax.all_to_all(jnp.stack(jax.lax.axis_size('dp') * [payload]), 'dp',...]
    all_to_all x0 -> x1, starting transfers between devices: none -> 14.4 us  [jax.lax.all_to_all(jnp.stack(jax.lax.axis_size('dp') * [payload]), 'dp',...]
where the time goes in v1:
time: 573 us; the launch traced here: 572 us
  waiting for transfers between devices  462 us (81%)
  local copies, waits for them, and re-layouts  34.6 us (6%)
  blocking collectives  23.5 us (4%)
  between operations  14.7 us (3%)
  starting transfers between devices  14.6 us (3%)
  matrix products  11.9 us (2%)
  other arithmetic  11 us (2%)
    reduce_scatter x1, waiting for transfers between devices, shards(): lax.psum_scatter(term + jnp.where(own_rows[:, None], carried, 0.0), 'dp',...  226 us
    psum x1, waiting for transfers between devices, shards(): lax.psum(partial_value.astype(jnp.bfloat16), 'blk').astype(jnp.float32)  102 us
    psum x1, waiting for transfers between devices, shards(): lax.psum(partial_units.astype(jnp.bfloat16), 'blk').astype(jnp.float32)  85.6 us
    all_to_all x1, waiting for transfers between devices, jax.lax.all_to_all(jnp.stack(jax.lax.axis_size('dp') * [payload]), 'dp',...  48.3 us
    psum x1, blocking collectives, shards(): lax.psum((jnp.sum(moved * moved, -1), jnp.sum(moved * weighted, -1)), 'blk')  23.5 us
    all_to_all x1, starting transfers between devices, jax.lax.all_to_all(jnp.stack(jax.lax.axis_size('dp') * [payload]), 'dp',...  14.4 us
  transfers between devices with their start and end apart: 4, of which 4 were waited for; matrix products, arithmetic and copies ran while one was open for 2% of the time, Pallas kernels for 0%

profile of v1, /device:TPU:8, one launch (start us, length us, event | category | flops | bytes accessed | tf_op | source)
XLA Modules:
  0.0 572.3 jit_solution(15055319768376023194)
XLA Ops:
  9.4 6.2 %gather_fusion = bf16[32,128,2,128]{3,2,1,0:T(2,128)(2,1)} fusion(bf16[32,128,2,128]{3,2,1,0:T(2,128)(2,1)S(1)} %bitcast.105, s32[1024]{0:T(1024)S(1)} %pad_clamp_fusion), kind=kCustom, calls=%fused_computation | custom fusion | bytes 4194432 | tf_op jit(solution)/shard_map/jit(_take)/gather | solution.py:22
  15.5 3.6 copy.69
  19.3 2.3 fusion.31
  22.7 2.0 broadcast_select_fusion
  24.7 1.3 copy-done.2
  27.9 1.6 fusion.11
  29.8 1.9 fusion.6
  31.8 0.9 convolution_convert_fusion.2
  33.6 102.2 %all-reduce.4.cloned.1.call-done = bf16[32,2048]{1,0:T(8,128)(2,1)} async-done(((bf16[32,2048]{1,0:T(8,128)(2,1)}), bf16[32,2048]{1,0:T(8,128)(2,1)}) %all-reduce.4.cloned.1.call-update) | async-done | bytes 131088 | tf_op jit(solution)/shard_map/psum | solution.py:99
  135.7 1.1 convert_add_fusion
  136.9 1.1 stack.2
  138.0 14.4 %all-to-all-start = ((bf16[64,32,256]{2,1,0:T(8,128)(2,1)}), bf16[64,32,256]{2,1,0:T(8,128)(2,1)S(1)}, u32[]{:S(2)}, u32[]{:S(2)}) async-start(bf16[64,32,256]{2,1,0:T(8,128)(2,1)} %stack.2), calls=%async_computation | async-start | bytes 2097152 | tf_op jit(solution)/shard_map/all_to_all | solution.py:12
  152.5 1.0 iota_add_fusion
  153.5 1.4 add.179
  154.9 1.3 add.163
  156.2 48.3 %all-to-all-done = bf16[64,32,256]{2,1,0:T(8,128)(2,1)S(1)} async-done(((bf16[64,32,256]{2,1,0:T(8,128)(2,1)}), bf16[64,32,256]{2,1,0:T(8,128)(2,1)S(1)}, u32[]{:S(2)}, u32[]{:S(2)}) %all-to-all-start) | async-done | bytes 1048608 | tf_op jit(solution)/shard_map/all_to_all | solution.py:12
  206.5 8.6 %gather_fusion.2 = f32[2048,256]{1,0:T(8,128)} fusion(f32[32,256]{1,0:T(8,128)S(1)} %get-tuple-element.7, s32[2048]{0:T(1024)S(1)} %broadcast_clamp_fusion), kind=kCustom, calls=%fused_computation.2 | custom fusion | bytes 4202496 | tf_op jit(solution)/shard_map/jit(_take)/gather | solution.py:126
  215.1 85.6 %all-reduce.6.cloned.1.call-done = bf16[2048,192]{0,1:T(8,128)(2,1)} async-done(((bf16[2048,192]{0,1:T(8,128)(2,1)}), bf16[2048,192]{0,1:T(8,128)(2,1)}) %all-reduce.6.cloned.1.call-update) | async-done | bytes 786448 | tf_op jit(solution)/shard_map/psum | solution.py:120
  300.7 1.3 convert_element_type.59
  302.5 6.2 %gather_fusion.1 = bf16[2048,96]{1,0:T(8,128)(2,1)S(1)} fusion(bf16[2048,96]{1,0:T(8,128)(2,1)S(1)} %copy.86, s32[2048]{0:T(1024)S(1)} %broadcast_clamp_fusion.1), kind=kCustom, calls=%fused_computation.1 | custom fusion | bytes 794624 | tf_op jit(solution)/shard_map/jit(_take)/gather | solution.py:123
  308.7 4.9 convolution_add_fusion
  314.2 226.0 %reduce-scatter.2.cloned.1.call-done = f32[32,256]{1,0:T(8,128)} async-done(((f32[2048,256]{1,0:T(8,128)}), f32[32,256]{1,0:T(8,128)}) %reduce-scatter.2.cloned.1.call-update) | async-done | bytes 32784 | tf_op jit(solution)/shard_map/reduce_scatter | solution.py:127
  540.2 1.5 multiply_reduce_fusion.1
  541.8 23.5 %all-reduce = (f32[32]{0:T(128)S(1)}, f32[32]{0:T(128)S(1)}) all-reduce(f32[32]{0:T(128)S(1)} %get-tuple-element.3, f32[32]{0:T(128)S(1)} %get-tuple-element.2), channel_id=1, replica_groups=mesh['dp'=64,'blk'=8] {'blk'}, use_global_device_ids=true, to_apply=%region_11.12 | all-reduce | flops 64 | bytes 512 | tf_op jit(solution)/shard_map/psum | solution.py:131
  (74 shorter events, 9.5 us)
Async XLA Ops:
  7.2 2.2 copy-start
  7.2 128.5 %all-reduce.4.cloned.1.call-start = ((), (), s32[]{:S(2)}) async-start(), calls=%async_computation.2 | async-start | bytes 262144 | tf_op jit(solution)/shard_map/psum | solution.py:99
  15.5 3.7 copy-start.11
  15.5 3.7 copy-start.1
  19.3 2.3 copy-start.14
  19.3 2.9 copy-start.9
  24.7 1.4 copy-start.2
  26.6 1.0 copy-start.4
  27.9 3.9 copy-start.3
  29.8 105.9 %copy-start.5 = (bf16[32,2048]{1,0:T(8,128)(2,1)S(1)}, bf16[32,2048]{1,0:T(8,128)(2,1)}, u32[]{:S(2)}) copy-start(bf16[32,2048]{1,0:T(8,128)(2,1)} %param.16) | copy-start | bytes 393220
  32.8 119.7 %copy-start.10 = (s32[1024]{0:T(1024)S(1)}, s32[1024]{0:T(1024)}, u32[]{:S(2)}) copy-start(s32[1024]{0:T(1024)} %param.24) | copy-start | bytes 12292
  138.0 66.5 %copy-start.7 = (bf16[256,96]{0,1:T(8,128)(2,1)S(1)}, bf16[256,96]{0,1:T(8,128)(2,1)}, u32[]{:S(2)}) copy-start(bf16[256,96]{0,1:T(8,128)(2,1)} %param.28) | copy-start | bytes 147460
  138.0 67.0 %copy-start.8 = (bf16[256,96]{0,1:T(8,128)(2,1)S(1)}, bf16[256,96]{0,1:T(8,128)(2,1)}, u32[]{:S(2)}) copy-start(bf16[256,96]{0,1:T(8,128)(2,1)} %param.27) | copy-start | bytes 147460
  138.0 66.5 %all-to-all-start = ((bf16[64,32,256]{2,1,0:T(8,128)(2,1)}), bf16[64,32,256]{2,1,0:T(8,128)(2,1)S(1)}, u32[]{:S(2)}, u32[]{:S(2)}) async-start(bf16[64,32,256]{2,1,0:T(8,128)(2,1)} %stack.2), calls=%async_computation | async-start | bytes 2097152 | tf_op jit(solution)/shard_map/all_to_all | solution.py:12
  152.4 148.2 %all-reduce.6.cloned.1.call-start = ((), (), s32[]{:S(2)}) async-start(), calls=%async_computation.3 | async-start | bytes 1572864 | tf_op jit(solution)/shard_map/psum | solution.py:120
  206.4 333.9 %reduce-scatter.2.cloned.1.call-start = ((), (), s32[]{:S(2)}) async-start(), calls=%async_computation.4 | async-start | bytes 2129920 | tf_op jit(solution)/shard_map/reduce_scatter | solution.py:127
  302.5 6.2 %copy-start.6 = (bf16[96,256]{1,0:T(8,128)(2,1)S(1)}, bf16[96,256]{1,0:T(8,128)(2,1)}, u32[]{:S(2)}) copy-start(bf16[96,256]{1,0:T(8,128)(2,1)} %param.29) | copy-start | bytes 147460
  313.6 0.7 copy-start.12
  313.6 0.7 copy-start.13
Sparse Core Ops, SparseCore 0:
  32.9 102.7 all-reduce.3
  206.5 94.1 all-reduce.5
  313.7 226.4 reduce-scatter.1
